TPU v7x, 32 devices: a whole 2x2x4 slice. The times are simulated.
32 devices in a mesh: fsdp: 2 (over y), rows: 8 (over z, core), cols: 2 (over x).
Axes of the slice: x: 2, y: 2, z: 4, core: 2. Of those that a mesh axis runs over, the one named last changes fastest.
Arguments:
- image: bfloat16 [2, 128, 256, 128], P('fsdp', 'rows', 'cols'), may hold values from -6 to 6
- dw_kernel: float32 [7, 7, 128], replicated, may hold values from -0.875 to 0.875
- dw_bias: float32 [128], replicated, may hold values from -3 to 3
- layer_norm_gain: float32 [128], replicated, may hold values from 0.1 to 1.9
- layer_norm_bias: float32 [128], replicated, may hold values from -3 to 3
- w_in: bfloat16 [128, 512], P('fsdp'), may hold values from -0.5 to 0.5
- b_in: float32 [512], replicated, may hold values from -3 to 3
- w_out: bfloat16 [512, 128], P('fsdp'), may hold values from -0.25 to 0.25
- b_out: float32 [128], replicated, may hold values from -3 to 3
- cotangent: bfloat16 [2, 128, 256, 128], P('fsdp', 'rows', 'cols'), may hold values from -60 to 60
Outputs:
- mixed: bfloat16 [2, 128, 256, 128], P('fsdp', 'rows', 'cols')
- d_image: bfloat16 [2, 128, 256, 128], P('fsdp', 'rows', 'cols')
- g_w_in: float32 [128, 512], P('fsdp')
- g_w_out: float32 [512, 128], P('fsdp')
- g_b_in: float32 [512], replicated
- g_kernel: float32 [7, 7, 128], replicated
- g_gain: float32 [128], replicated
All inputs are finite; a program needn't handle non-finite values.
Results may differ from a plain program's by a relative error of at most 0.0057.
Values may be sent and summed in bfloat16 or wider, within the bound.
No kernel may reach another device: no remote copies, remote signals or barrier semaphores. Data moves between devices by JAX's collectives and lax.ppermute only.
A program may use at most 64 MiB of HBM per device.

v0:
```python
import math
import jax
import jax.numpy as jnp
from jax import lax
from jax.sharding import PartitionSpec as P

norm_eps = 1e-06
gelu_coef = math.sqrt(2.0 / math.pi)
cubic_coef = 0.044715


def padded_2(shard, sides, width):
    for axis, dim in sides:
        devices, length = (lax.axis_size(axis), shard.shape[dim])
        up = [(i, (i + 1) % devices) for i in range(devices - 1)]
        down = [(j, i) for i, j in up]
        last = lax.slice_in_dim(shard, length - width, length, axis=dim)
        leading = lax.slice_in_dim(shard, 0, width, axis=dim)
        before = lax.ppermute(last, axis, up)
        after = lax.ppermute(leading, axis, down)
        shard = jnp.concatenate([before, shard, after], axis=dim)
    return shard


def depthwise_taps(padded, kernel, height, width):
    total = jnp.zeros((height, width, padded.shape[2]), jnp.float32)
    for row_tap in range(7):
        for col_tap in range(7):
            total = (
                total
                + padded[row_tap : row_tap + height, col_tap : col_tap + width]
                * kernel[row_tap, col_tap]
            )
    return total


def transposed_taps(padded, kernel, height, width):
    total = jnp.zeros((height, width, padded.shape[2]), jnp.float32)
    for row_tap in range(7):
        for col_tap in range(7):
            total = (
                total
                + padded[6 - row_tap : 6 - row_tap + height, 6 - col_tap : 6 - col_tap + width]
                * kernel[row_tap, col_tap]
            )
    return total


def gelu_parts(pre):
    inner = gelu_coef * (pre + cubic_coef * pre * pre * pre)
    tanh_val = jnp.tanh(inner)
    value = 0.5 * pre * (1.0 + tanh_val)
    slope = 0.5 * (1.0 + tanh_val) + 0.5 * pre * (1.0 - tanh_val * tanh_val) * gelu_coef * (
        1.0 + 3.0 * cubic_coef * pre * pre
    )
    return (value, slope)


def extend_image(field):
    return padded_2(field, (("rows", 0), ("cols", 1)), 3)


def extend_grad(field):
    return padded_2(field, (("rows", 0), ("cols", 1)), 3)


def on_device(
    image, dw_kernel, dw_bias, layer_norm_gain, layer_norm_bias, w_in, b_in, w_out, b_out, cotangent
):
    contract_rows = (((0,), (0,)), ((), ()))
    contract_cols = (((1,), (1,)), ((), ()))
    field = image[0]
    upstream = cotangent[0]
    height, width, channel_count = field.shape
    padded_f = extend_image(field).astype(jnp.float32)
    conv = depthwise_taps(padded_f, dw_kernel, height, width) + dw_bias
    center = jnp.mean(conv, axis=-1, keepdims=True)
    variance_spread = conv - center
    inverse_deviation = lax.rsqrt(
        jnp.mean(variance_spread * variance_spread, axis=-1, keepdims=True) + norm_eps
    )
    standardized_input = variance_spread * inverse_deviation
    normalized_input = (
        (standardized_input * layer_norm_gain + layer_norm_bias)
        .astype(jnp.bfloat16)
        .reshape(-1, channel_count)
    )
    full_in, full_out = (
        lax.all_gather(w_in, "fsdp", axis=0, tiled=True),
        lax.all_gather(w_out, "fsdp", axis=0, tiled=True),
    )
    pre = jnp.dot(normalized_input, full_in, preferred_element_type=jnp.float32) + b_in
    value, slope = gelu_parts(pre)
    hidden = value.astype(jnp.bfloat16)
    mixed = (
        field.reshape(-1, channel_count).astype(jnp.float32)
        + jnp.dot(hidden, full_out, preferred_element_type=jnp.float32)
        + b_out
    )
    mixed = mixed.astype(jnp.bfloat16).reshape(height, width, channel_count)
    flat_up = upstream.reshape(-1, channel_count)
    d_hidden = lax.dot_general(flat_up, full_out, contract_cols, preferred_element_type=jnp.float32)
    d_pre = (d_hidden * slope).astype(jnp.bfloat16)
    normalized_gradient = lax.dot_general(
        d_pre, full_in, contract_cols, preferred_element_type=jnp.float32
    ).reshape(height, width, channel_count)
    gain_product = jnp.sum(normalized_gradient * standardized_input, axis=(0, 1))
    centered_scaled_gradient = normalized_gradient * layer_norm_gain
    convolution_gradient = (
        inverse_deviation
        * (
            centered_scaled_gradient
            - jnp.mean(centered_scaled_gradient, axis=-1, keepdims=True)
            - standardized_input
            * jnp.mean(centered_scaled_gradient * standardized_input, axis=-1, keepdims=True)
        )
    ).astype(jnp.bfloat16)
    bias_term = jnp.sum(d_pre.astype(jnp.float32), axis=0)
    grad_padded = extend_grad(convolution_gradient).astype(jnp.float32)
    d_image = (
        upstream.astype(jnp.float32) + transposed_taps(grad_padded, dw_kernel, height, width)
    ).astype(jnp.bfloat16)
    conv_grad = convolution_gradient.astype(jnp.float32)
    kernel_rows = []
    for row_tap in range(7):
        for col_tap in range(7):
            kernel_rows.append(
                jnp.sum(
                    padded_f[row_tap : row_tap + height, col_tap : col_tap + width] * conv_grad,
                    axis=(0, 1),
                )
            )
    kernel_term = jnp.stack(kernel_rows).reshape(7, 7, channel_count)
    in_rows = w_in.shape[0]
    out_rows = w_out.shape[0]
    term_in = lax.dot_general(
        normalized_input, d_pre, contract_rows, preferred_element_type=jnp.float32
    )
    term_out = lax.dot_general(hidden, flat_up, contract_rows, preferred_element_type=jnp.float32)
    total_in, total_out, g_b_in, g_kernel, g_gain = lax.psum(
        (term_in, term_out, bias_term, kernel_term, gain_product), ("fsdp", "rows", "cols")
    )
    owner = lax.axis_index("fsdp")
    g_w_in = lax.dynamic_slice_in_dim(total_in, owner * in_rows, in_rows, 0)
    g_w_out = lax.dynamic_slice_in_dim(total_out, owner * out_rows, out_rows, 0)
    return (mixed[None], d_image[None], g_w_in, g_w_out, g_b_in, g_kernel, g_gain)


def solution(mesh):
    return jax.shard_map(
        on_device,
        mesh=mesh,
        in_specs=(
            P("fsdp", "rows", "cols", None),
            P(),
            P(),
            P(),
            P(),
            P("fsdp", None),
            P(),
            P("fsdp", None),
            P(),
            P("fsdp", "rows", "cols", None),
        ),
        out_specs=(
            P("fsdp", "rows", "cols", None),
            P("fsdp", "rows", "cols", None),
            P("fsdp", None),
            P("fsdp", None),
            P(),
            P(),
            P(),
        ),
        check_vma=False,
    )
```

profile of v0, /device:TPU:0, one launch (start us, length us, event | category | flops | bytes accessed | tf_op | source)
XLA Modules:
  0.0 208.9 jit_solution(18088232705827283579)
XLA Ops:
  8.2 2.4 %collective-permute-start = (bf16[3,128,128]{2,1,0:T(8,128)(2,1)S(1)}, bf16[3,128,128]{2,1,0:T(8,128)(2,1)S(1)}, u32[]{:S(2)}, u32[]{:S(2)}) collective-permute-start(bf16[3,128,128]{2,1,0:T(8,128)(2,1)S(1)} %get-tuple-element.72), channel_id=1, source_target_pairs={{0,2},{2,4},{4,6},{6,8},{8,10},{10,12},{12,14},{1,3},{3,5},{5,7},{... | collective-permute-start | bytes 294920 | tf_op jit(solution)/shard_map/ppermute | solution.py:19
  10.6 1.3 collective-permute-start.1
  14.8 5.5 %all_gather.6 = bf16[128,512]{1,0:T(8,128)(2,1)S(1)} all-gather(bf16[64,512]{1,0:T(8,128)(2,1)} %param.15), channel_id=1, replica_groups=mesh['fsdp'=2,'rows'=8,'cols'=2] {'fsdp'}, dimensions={0}, use_global_device_ids=true | all-gather | bytes 196608 | tf_op jit(solution)/shard_map/all_gather | solution.py:89
  21.1 3.8 %collective-permute-start.2 = (bf16[22,3,128]{2,1,0:T(4,128)(2,1)S(1)}, bf16[22,3,128]{2,1,0:T(4,128)(2,1)S(1)}, u32[]{:S(2)}, u32[]{:S(2)}) collective-permute-start(bf16[22,3,128]{2,1,0:T(4,128)(2,1)S(1)} %get-tuple-element.68), channel_id=1, source_target_pairs={{0,1},{2,3},{4,5},{6,7},{8,9},{10,11},{12,13},{14,15},{16,17},{18,... | collective-permute-start | bytes 50696 | tf_op jit(solution)/shard_map/ppermute | solution.py:19
  25.0 1.3 collective-permute-start.3
  26.3 5.8 %all_gather.7 = bf16[512,128]{1,0:T(8,128)(2,1)S(1)} all-gather(bf16[256,128]{1,0:T(8,128)(2,1)} %param.17), channel_id=1, replica_groups=mesh['fsdp'=2,'rows'=8,'cols'=2] {'fsdp'}, dimensions={0}, use_global_device_ids=true | all-gather | bytes 196608 | tf_op jit(solution)/shard_map/all_gather | solution.py:90
  33.3 8.2 %fusion.109 = (f32[16,128]{1,0:T(8,128)S(1)}, f32[16,128,128]{2,1,0:T(8,128)S(1)}) fusion(f32[128]{0:T(128)} %param.12, f32[128]{0:T(128)S(1)} %get-tuple-element.121, f32[22,134,128]{2,1,0:T(8,128)S(1)} %maximum_convert_fusion, f32[128]{0:T(128)S(1)} %get-tuple-element.122, f32[128]{0:T(128)S(1)} %get-tuple-element.75, f32[128]{0:T(128)S(1)} %get-tuple-element.76, ...), kind=kLoop, calls=%fused_computation.285 | loop fusion | flops 25950208 | bytes 52462592 | tf_op jit(solution)/shard_map/reduce_sum | solution.py:77
  42.9 1.8 multiply_convert_fusion
  44.7 3.1 %convert_reduce_fusion = (f32[512]{0:T(512)S(1)}, bf16[2048,512]{1,0:T(8,128)(2,1)S(1)}) fusion(f32[2048,512]{1,0:T(8,128)S(1)} %get-tuple-element.124, f32[512]{0:T(512)S(1)} %copy-done.7, bf16[2048,128]{1,0:T(8,128)(2,1)S(1)} %bitcast.186, bf16[512,128]{1,0:T(8,128)(2,1)S(1)} %all_gather.7), kind=kOutput, calls=%fused_computation.58 | convolution fusion | flops 291503616 | bytes 6950912 | tf_op jit(solution)/shard_map/dot_general | solution.py:102
  49.7 3.0 %fusion.56 = (f32[128]{0:T(128)S(1)}, f32[128]{0:T(128)S(1)}, f32[128]{0:T(128)S(1)}, f32[128]{0:T(128)S(1)}, f32[128]{0:T(128)S(1)}, /*index=5*/f32[128]{0:T(12...) fusion(f32[22,134,128]{2,1,0:T(8,128)S(1)} %maximum_convert_fus, ...), kind=kLoop, calls=%fused_computation.110 | loop fusion | flops 11794176 | bytes 21538304 | tf_op jit(solution)/shard_map/reduce_sum | solution.py:128
  52.7 2.4 %fusion.57 = (f32[128]{0:T(128)S(1)}, f32[128]{0:T(128)S(1)}, f32[128]{0:T(128)S(1)}, f32[128]{0:T(128)S(1)}, f32[128]{0:T(128)S(1)}, /*index=5*/f32[128]{0:T(12...) fusion(bf16[16,128,128]{2,1,0:T(8,128)(2,1)S(1)} %get-tuple-ele, ...), kind=kLoop, calls=%fused_computation.111 | loop fusion | flops 9697024 | bytes 19407872 | tf_op jit(solution)/shard_map/reduce_sum | solution.py:128
  55.1 1.7 fusion.55
  58.0 2.0 collective-permute-start.4
  60.1 1.3 collective-permute-start.5
  61.4 1.5 fusion.112
  62.9 3.4 %collective-permute-done.5 = bf16[3,128,128]{2,1,0:T(8,128)(2,1)S(1)} collective-permute-done((bf16[3,128,128]{2,1,0:T(8,128)(2,1)S(1)}, bf16[3,128,128]{2,1,0:T(8,128)(2,1)S(1)}, u32[]{:S(2)}, u32[]{:S(2)}) %collective-permute-start.5) | collective-permute-done | bytes 98336 | tf_op jit(solution)/shard_map/ppermute | solution.py:20
  66.3 4.5 %collective-permute-start.6 = (bf16[22,3,128]{2,1,0:T(4,128)(2,1)S(1)}, bf16[22,3,128]{2,1,0:T(4,128)(2,1)S(1)}, u32[]{:S(2)}, u32[]{:S(2)}) collective-permute-start(bf16[22,3,128]{2,1,0:T(4,128)(2,1)S(1)} %get-tuple-element.66), channel_id=1, source_target_pairs={{0,1},{2,3},{4,5},{6,7},{8,9},{10,11},{12,13},{14,15},{16,17},{18,... | collective-permute-start | bytes 50696 | tf_op jit(solution)/shard_map/ppermute | solution.py:19
  70.8 1.5 collective-permute-start.7
  72.3 3.1 %fusion.8 = bf16[2048,128]{1,0:T(8,128)(2,1)} fusion(bf16[2048,512]{1,0:T(8,128)(2,1)} %copy-done, bf16[512,128]{1,0:T(8,128)(2,1)S(1)} %all_gather.7, bf16[2048,128]{1,0:T(8,128)(2,1)S(1)} %bitcast.185, f32[128]{0:T(128)S(1)} %copy-done.6), kind=kOutput, calls=%fused_computation.62 | convolution fusion | flops 269484032 | bytes 3277312 | tf_op jit(solution)/shard_map/dot_general | solution.py:97
  75.5 43.9 %all-reduce = (f32[512]{0:T(512)}, f32[7,7,128]{2,1,0:T(8,128)}, f32[128]{0:T(128)}) all-reduce(f32[512]{0:T(512)S(1)} %get-tuple-element.127, f32[7,7,128]{2,1,0:T(8,128)S(1)} %reshape.62, f32[128]{0:T(128)S(1)} %get-tuple-element.56), channel_id=1, replica_groups=mesh['fsdp'=2,'rows'=8,'cols'=2] {'fsdp','rows','cols'}, use_global_device_ids=true, to_apply=%region_7.0 | all-reduce | flops 6912 | bytes 55296 | tf_op jit(solution)/shard_map/psum | solution.py:140
  119.7 8.1 %fusion.108 = bf16[1,16,128,128]{3,2,1,0:T(8,128)(2,1)} fusion(f32[128]{0:T(128)S(1)} %get-tuple-element.121, f32[22,134,128]{2,1,0:T(8,128)S(1)} %maximum_convert_fusion.1, f32[128]{0:T(128)S(1)} %get-tuple-element.122, f32[128]{0:T(128)S(1)} %get-tuple-element.75, f32[128]{0:T(128)S(1)} %get-tuple-element.76, f32[128]{0:T(128)S(1)} %get-tuple-element.77, ...), kind=kLoop, calls=%fused_computation.221 | loop fusion | flops 26214400 | bytes 52453888 | tf_op jit(solution)/shard_map/broadcast_in_dim | solution.py:146
  127.9 71.1 %all-reduce.4.cloned.1.call-done = (f32[128,512]{1,0:T(8,128)}, f32[512,128]{1,0:T(8,128)}) async-done(((f32[128,512]{1,0:T(8,128)}, f32[512,128]{1,0:T(8,128)}), (f32[128,512]{1,0:T(8,128)}, f32[512,128]{1,0:T(8,128)})) %all-reduce.4.cloned.1.call-update) | async-done | bytes 524304 | tf_op jit(solution)/shard_map/psum | solution.py:140
  199.0 1.6 constant_dynamic-slice_fusion
  200.5 1.6 constant_dynamic-slice_fusion.1
  (45 shorter events, 10.6 us)
Async XLA Ops:
  7.2 191.8 %all-reduce.4.cloned.1.call-start = ((), (), s32[]{:S(2)}) async-start(), calls=%async_computation | async-start | bytes 1048576 | tf_op jit(solution)/shard_map/psum | solution.py:140
  8.2 12.1 %collective-permute-start = (bf16[3,128,128]{2,1,0:T(8,128)(2,1)S(1)}, bf16[3,128,128]{2,1,0:T(8,128)(2,1)S(1)}, u32[]{:S(2)}, u32[]{:S(2)}) collective-permute-start(bf16[3,128,128]{2,1,0:T(8,128)(2,1)S(1)} %get-tuple-element.72), channel_id=1, source_target_pairs={{0,2},{2,4},{4,6},{6,8},{8,10},{10,12},{12,14},{1,3},{3,5},{5,7},{... | collective-permute-start | bytes 294920 | tf_op jit(solution)/shard_map/ppermute | solution.py:19
  10.6 9.7 %collective-permute-start.1 = (bf16[3,128,128]{2,1,0:T(8,128)(2,1)S(1)}, bf16[3,128,128]{2,1,0:T(8,128)(2,1)S(1)}, u32[]{:S(2)}, u32[]{:S(2)}) collective-permute-start(bf16[3,128,128]{2,1,0:T(8,128)(2,1)S(1)} %get-tuple-element.73), channel_id=1, source_target_pairs={{2,0},{4,2},{6,4},{8,6},{10,8},{12,10},{14,12},{3,1},{5,3},{7,5},{... | collective-permute-start | bytes 294920 | tf_op jit(solution)/shard_map/ppermute | solution.py:20
  21.1 10.9 %collective-permute-start.2 = (bf16[22,3,128]{2,1,0:T(4,128)(2,1)S(1)}, bf16[22,3,128]{2,1,0:T(4,128)(2,1)S(1)}, u32[]{:S(2)}, u32[]{:S(2)}) collective-permute-start(bf16[22,3,128]{2,1,0:T(4,128)(2,1)S(1)} %get-tuple-element.68), channel_id=1, source_target_pairs={{0,1},{2,3},{4,5},{6,7},{8,9},{10,11},{12,13},{14,15},{16,17},{18,... | collective-permute-start | bytes 50696 | tf_op jit(solution)/shard_map/ppermute | solution.py:19
  25.0 7.1 %collective-permute-start.3 = (bf16[22,3,128]{2,1,0:T(4,128)(2,1)S(1)}, bf16[22,3,128]{2,1,0:T(4,128)(2,1)S(1)}, u32[]{:S(2)}, u32[]{:S(2)}) collective-permute-start(bf16[22,3,128]{2,1,0:T(4,128)(2,1)S(1)} %get-tuple-element.69), channel_id=1, source_target_pairs={{1,0},{3,2},{5,4},{7,6},{9,8},{11,10},{13,12},{15,14},{17,16},{19,... | collective-permute-start | bytes 50696 | tf_op jit(solution)/shard_map/ppermute | solution.py:20
  33.3 8.9 %copy-start.4 = (f32[128]{0:T(128)S(1)}, f32[128]{0:T(128)}, u32[]{:S(2)}) copy-start(f32[128]{0:T(128)} %param.13) | copy-start | bytes 1540
  33.3 8.9 %copy-start.5 = (f32[128]{0:T(128)S(1)}, f32[128]{0:T(128)}, u32[]{:S(2)}) copy-start(f32[128]{0:T(128)} %param.14) | copy-start | bytes 1540
  33.3 9.5 %copy-start.7 = (f32[512]{0:T(512)S(1)}, f32[512]{0:T(512)}, u32[]{:S(2)}) copy-start(f32[512]{0:T(512)} %param.16) | copy-start | bytes 6148
  42.9 1.8 copy-start.2
  44.7 16.7 %copy-start = (bf16[2048,512]{1,0:T(8,128)(2,1)}, bf16[2048,512]{1,0:T(8,128)(2,1)S(1)}, u32[]{:S(2)}) copy-start(bf16[2048,512]{1,0:T(8,128)(2,1)S(1)} %get-tuple-element.123) | copy-start | bytes 6291460
  56.8 15.5 %copy-start.1 = (bf16[1,16,128,128]{3,2,1,0:T(8,128)(2,1)S(1)}, bf16[1,16,128,128]{3,2,1,0:T(8,128)(2,1)}, u32[]{:S(2)}) copy-start(bf16[1,16,128,128]{3,2,1,0:T(8,128)(2,1)} %param.10) | copy-start | bytes 1572868
  56.8 15.5 %copy-start.6 = (f32[128]{0:T(128)S(1)}, f32[128]{0:T(128)}, u32[]{:S(2)}) copy-start(f32[128]{0:T(128)} %param.18) | copy-start | bytes 1540
  58.0 4.8 %collective-permute-start.4 = (bf16[3,128,128]{2,1,0:T(8,128)(2,1)S(1)}, bf16[3,128,128]{2,1,0:T(8,128)(2,1)S(1)}, u32[]{:S(2)}, u32[]{:S(2)}) collective-permute-start(bf16[3,128,128]{2,1,0:T(8,128)(2,1)S(1)} %get-tuple-element.70), channel_id=1, source_target_pairs={{0,2},{2,4},{4,6},{6,8},{8,10},{10,12},{12,14},{1,3},{3,5},{5,7},{... | collective-permute-start | bytes 294920 | tf_op jit(solution)/shard_map/ppermute | solution.py:19
  60.1 6.2 %collective-permute-start.5 = (bf16[3,128,128]{2,1,0:T(8,128)(2,1)S(1)}, bf16[3,128,128]{2,1,0:T(8,128)(2,1)S(1)}, u32[]{:S(2)}, u32[]{:S(2)}) collective-permute-start(bf16[3,128,128]{2,1,0:T(8,128)(2,1)S(1)} %get-tuple-element.71), channel_id=1, source_target_pairs={{2,0},{4,2},{6,4},{8,6},{10,8},{12,10},{14,12},{3,1},{5,3},{7,5},{... | collective-permute-start | bytes 294920 | tf_op jit(solution)/shard_map/ppermute | solution.py:20
  62.8 56.9 %copy-start.3 = (bf16[1,16,128,128]{3,2,1,0:T(8,128)(2,1)S(1)}, bf16[1,16,128,128]{3,2,1,0:T(8,128)(2,1)}, u32[]{:S(2)}) copy-start(bf16[1,16,128,128]{3,2,1,0:T(8,128)(2,1)} %param.19) | copy-start | bytes 1572868
  66.3 53.2 %collective-permute-start.6 = (bf16[22,3,128]{2,1,0:T(4,128)(2,1)S(1)}, bf16[22,3,128]{2,1,0:T(4,128)(2,1)S(1)}, u32[]{:S(2)}, u32[]{:S(2)}) collective-permute-start(bf16[22,3,128]{2,1,0:T(4,128)(2,1)S(1)} %get-tuple-element.66), channel_id=1, source_target_pairs={{0,1},{2,3},{4,5},{6,7},{8,9},{10,11},{12,13},{14,15},{16,17},{18,... | collective-permute-start | bytes 50696 | tf_op jit(solution)/shard_map/ppermute | solution.py:19
  70.8 48.7 %collective-permute-start.7 = (bf16[22,3,128]{2,1,0:T(4,128)(2,1)S(1)}, bf16[22,3,128]{2,1,0:T(4,128)(2,1)S(1)}, u32[]{:S(2)}, u32[]{:S(2)}) collective-permute-start(bf16[22,3,128]{2,1,0:T(4,128)(2,1)S(1)} %get-tuple-element.67), channel_id=1, source_target_pairs={{1,0},{3,2},{5,4},{7,6},{9,8},{11,10},{13,12},{15,14},{17,16},{19,... | collective-permute-start | bytes 50696 | tf_op jit(solution)/shard_map/ppermute | solution.py:20
Sparse Core Ops, SparseCore 0:
  63.0 135.9 all-reduce.3
where the time goes:
time: 210 us; the launch traced here: 209 us
  waiting for transfers between devices  74.5 us (35%)
  blocking collectives  55.2 us (26%)
  other arithmetic  28 us (13%)
  starting transfers between devices  18.2 us (9%)
  between operations  14.4 us (7%)
  matrix products  11.5 us (5%)
  local copies, waits for them, and re-layouts  7.18 us (3%)
    psum x1, waiting for transfers between devices, on_device(): lax.psum((term_in, term_out, bias_term, kernel_term, gain_product), ('fsd...  71.1 us
    psum x1, blocking collectives, on_device(): lax.psum((term_in, term_out, bias_term, kernel_term, gain_product), ('fsd...  43.9 us
    ppermute x4, starting transfers between devices, padded_2(): before = lax.ppermute(last, axis, up)  12.8 us
    reduce_sum x1, other arithmetic, on_device(): center = jnp.mean(conv, axis=-1, keepdims=True)  8.22 us
    broadcast_in_dim x1, other arithmetic, on_device(): d_image[None]  8.14 us
    reduce_sum x3, other arithmetic, on_device(): jnp.sum(padded_f[row_tap:row_tap + height, col_tap:col_tap + width] * con...  7.12 us
    all_gather x1, blocking collectives, on_device(): lax.all_gather(w_out, 'fsdp', axis=0, tiled=True)  5.77 us
    all_gather x1, blocking collectives, on_device(): lax.all_gather(w_in, 'fsdp', axis=0, tiled=True)  5.51 us
  transfers between devices with their start and end apart: 9, of which 2 were waited for; matrix products, arithmetic and copies ran while one was open for 8% of the time, Pallas kernels for 0%

commit v1 on v0

--- a/solution.py
+++ b/solution.py
@@ -137,8 +137,13 @@
         normalized_input, d_pre, contract_rows, preferred_element_type=jnp.float32
     )
     term_out = lax.dot_general(hidden, flat_up, contract_rows, preferred_element_type=jnp.float32)
-    total_in, total_out, g_b_in, g_kernel, g_gain = lax.psum(
-        (term_in, term_out, bias_term, kernel_term, gain_product), ("fsdp", "rows", "cols")
+
+    def follow_kinds(frame_in):
+        state_next = jax.lax.psum(frame_in, ("rows", "cols"))
+        return jax.lax.psum(state_next, "fsdp")
+
+    total_in, total_out, g_b_in, g_kernel, g_gain = follow_kinds(
+        (term_in, term_out, bias_term, kernel_term, gain_product)
     )
     owner = lax.axis_index("fsdp")
     g_w_in = lax.dynamic_slice_in_dim(total_in, owner * in_rows, in_rows, 0)

time: 210 us -> 202 us (0.962)
  waiting for transfers between devices: 74.5 us -> 40.2 us
  blocking collectives: 55.2 us -> 82.3 us
    psum x1 -> x2, waiting for transfers between devices: 71.1 us -> 36.8 us  [the longest x1 23.4 us: follow_kinds(): return jax.lax.psum(state_next, 'fsdp')]
    psum x1 -> x2, blocking collectives: 43.9 us -> 71 us  [the longest x1 62.1 us: follow_kinds(): state_next = jax.lax.psum(frame_in, ('rows', 'cols'))]
  transfers between devices with their start and end apart: 9 -> 10, of which waited for: 2 -> 3; matrix products, arithmetic and copies ran while one was open for 8% -> 8% of each run, Pallas kernels for 0% -> 0%
where the time goes in v1:
time: 202 us
  blocking collectives  82.3 us (41%)
  waiting for transfers between devices  40.2 us (20%)
  other arithmetic  28 us (14%)
  starting transfers between devices  18.2 us (9%)
  between operations  14.4 us (7%)
  matrix products  11.4 us (6%)
  local copies, waits for them, and re-layouts  7.18 us (4%)
    psum x1, blocking collectives, follow_kinds(): state_next = jax.lax.psum(frame_in, ('rows', 'cols'))  62.1 us
    psum x1, waiting for transfers between devices, follow_kinds(): return jax.lax.psum(state_next, 'fsdp')  23.4 us
    psum x1, waiting for transfers between devices, follow_kinds(): state_next = jax.lax.psum(frame_in, ('rows', 'cols'))  13.4 us
    ppermute x4, starting transfers between devices, padded_2(): before = lax.ppermute(last, axis, up)  13 us
    psum x1, blocking collectives, follow_kinds(): return jax.lax.psum(state_next, 'fsdp')  8.96 us
    reduce_sum x1, other arithmetic, on_device(): center = jnp.mean(conv, axis=-1, keepdims=True)  8.22 us
    broadcast_in_dim x1, other arithmetic, on_device(): d_image[None]  8.14 us
    reduce_sum x3, other arithmetic, on_device(): jnp.sum(padded_f[row_tap:row_tap + height, col_tap:col_tap + width] * con...  7.12 us
  transfers between devices with their start and end apart: 10, of which 3 were waited for; matrix products, arithmetic and copies ran while one was open for 8% of the time, Pallas kernels for 0%

profile of v1, /device:TPU:0, one launch (start us, length us, event | category | flops | bytes accessed | tf_op | source)
XLA Modules:
  0.0 201.8 jit_solution(14206072131309521005)
XLA Ops:
  8.2 2.4 %collective-permute-start = (bf16[3,128,128]{2,1,0:T(8,128)(2,1)S(1)}, bf16[3,128,128]{2,1,0:T(8,128)(2,1)S(1)}, u32[]{:S(2)}, u32[]{:S(2)}) collective-permute-start(bf16[3,128,128]{2,1,0:T(8,128)(2,1)S(1)} %get-tuple-element.77), channel_id=1, source_target_pairs={{0,2},{2,4},{4,6},{6,8},{8,10},{10,12},{12,14},{1,3},{3,5},{5,7},{... | collective-permute-start | bytes 294920 | tf_op jit(solution)/shard_map/ppermute | solution.py:19
  14.8 5.5 %all_gather.6 = bf16[128,512]{1,0:T(8,128)(2,1)S(1)} all-gather(bf16[64,512]{1,0:T(8,128)(2,1)} %param.15), channel_id=1, replica_groups=mesh['fsdp'=2,'rows'=8,'cols'=2] {'fsdp'}, dimensions={0}, use_global_device_ids=true | all-gather | bytes 196608 | tf_op jit(solution)/shard_map/all_gather | solution.py:89
  21.1 3.8 %collective-permute-start.2 = (bf16[22,3,128]{2,1,0:T(4,128)(2,1)S(1)}, bf16[22,3,128]{2,1,0:T(4,128)(2,1)S(1)}, u32[]{:S(2)}, u32[]{:S(2)}) collective-permute-start(bf16[22,3,128]{2,1,0:T(4,128)(2,1)S(1)} %get-tuple-element.73), channel_id=1, source_target_pairs={{0,1},{2,3},{4,5},{6,7},{8,9},{10,11},{12,13},{14,15},{16,17},{18,... | collective-permute-start | bytes 50696 | tf_op jit(solution)/shard_map/ppermute | solution.py:19
  25.0 1.3 collective-permute-start.3
  26.3 5.8 %all_gather.7 = bf16[512,128]{1,0:T(8,128)(2,1)S(1)} all-gather(bf16[256,128]{1,0:T(8,128)(2,1)} %param.17), channel_id=1, replica_groups=mesh['fsdp'=2,'rows'=8,'cols'=2] {'fsdp'}, dimensions={0}, use_global_device_ids=true | all-gather | bytes 196608 | tf_op jit(solution)/shard_map/all_gather | solution.py:90
  33.3 8.2 %fusion.109 = (f32[16,128]{1,0:T(8,128)S(1)}, f32[16,128,128]{2,1,0:T(8,128)S(1)}) fusion(f32[128]{0:T(128)} %param.12, f32[128]{0:T(128)S(1)} %get-tuple-element.126, f32[22,134,128]{2,1,0:T(8,128)S(1)} %maximum_convert_fusion, f32[128]{0:T(128)S(1)} %get-tuple-element.127, f32[128]{0:T(128)S(1)} %get-tuple-element.80, f32[128]{0:T(128)S(1)} %get-tuple-element.81, ...), kind=kLoop, calls=%fused_computation.285 | loop fusion | flops 25950208 | bytes 52462592 | tf_op jit(solution)/shard_map/reduce_sum | solution.py:77
  42.9 1.8 multiply_convert_fusion
  44.7 3.1 %convert_reduce_fusion = (f32[512]{0:T(512)S(1)}, bf16[2048,512]{1,0:T(8,128)(2,1)S(1)}) fusion(f32[2048,512]{1,0:T(8,128)S(1)} %get-tuple-element.129, f32[512]{0:T(512)S(1)} %copy-done.7, bf16[2048,128]{1,0:T(8,128)(2,1)S(1)} %bitcast.186, bf16[512,128]{1,0:T(8,128)(2,1)S(1)} %all_gather.7), kind=kOutput, calls=%fused_computation.58 | convolution fusion | flops 291503616 | bytes 6950912 | tf_op jit(solution)/shard_map/dot_general | solution.py:102
  49.7 3.0 %fusion.56 = (f32[128]{0:T(128)S(1)}, f32[128]{0:T(128)S(1)}, f32[128]{0:T(128)S(1)}, f32[128]{0:T(128)S(1)}, f32[128]{0:T(128)S(1)}, /*index=5*/f32[128]{0:T(12...) fusion(f32[22,134,128]{2,1,0:T(8,128)S(1)} %maximum_convert_fus, ...), kind=kLoop, calls=%fused_computation.110 | loop fusion | flops 11794176 | bytes 21538304 | tf_op jit(solution)/shard_map/reduce_sum | solution.py:128
  52.7 2.4 %fusion.57 = (f32[128]{0:T(128)S(1)}, f32[128]{0:T(128)S(1)}, f32[128]{0:T(128)S(1)}, f32[128]{0:T(128)S(1)}, f32[128]{0:T(128)S(1)}, /*index=5*/f32[128]{0:T(12...) fusion(bf16[16,128,128]{2,1,0:T(8,128)(2,1)S(1)} %get-tuple-ele, ...), kind=kLoop, calls=%fused_computation.111 | loop fusion | flops 9697024 | bytes 19407872 | tf_op jit(solution)/shard_map/reduce_sum | solution.py:128
  55.1 1.7 fusion.55
  58.0 2.0 %collective-permute-start.4 = (bf16[3,128,128]{2,1,0:T(8,128)(2,1)S(1)}, bf16[3,128,128]{2,1,0:T(8,128)(2,1)S(1)}, u32[]{:S(2)}, u32[]{:S(2)}) collective-permute-start(bf16[3,128,128]{2,1,0:T(8,128)(2,1)S(1)} %get-tuple-element.75), channel_id=1, source_target_pairs={{0,2},{2,4},{4,6},{6,8},{8,10},{10,12},{12,14},{1,3},{3,5},{5,7},{... | collective-permute-start | bytes 294920 | tf_op jit(solution)/shard_map/ppermute | solution.py:19
  61.4 1.5 fusion.112
  62.9 3.3 %collective-permute-done.5 = bf16[3,128,128]{2,1,0:T(8,128)(2,1)S(1)} collective-permute-done((bf16[3,128,128]{2,1,0:T(8,128)(2,1)S(1)}, bf16[3,128,128]{2,1,0:T(8,128)(2,1)S(1)}, u32[]{:S(2)}, u32[]{:S(2)}) %collective-permute-start.5) | collective-permute-done | bytes 98336 | tf_op jit(solution)/shard_map/ppermute | solution.py:20
  66.3 4.7 %collective-permute-start.6 = (bf16[22,3,128]{2,1,0:T(4,128)(2,1)S(1)}, bf16[22,3,128]{2,1,0:T(4,128)(2,1)S(1)}, u32[]{:S(2)}, u32[]{:S(2)}) collective-permute-start(bf16[22,3,128]{2,1,0:T(4,128)(2,1)S(1)} %get-tuple-element.71), channel_id=1, source_target_pairs={{0,1},{2,3},{4,5},{6,7},{8,9},{10,11},{12,13},{14,15},{16,17},{18,... | collective-permute-start | bytes 50696 | tf_op jit(solution)/shard_map/ppermute | solution.py:19
  71.0 1.3 collective-permute-start.7
  72.3 3.1 %fusion.8 = bf16[2048,128]{1,0:T(8,128)(2,1)} fusion(bf16[2048,512]{1,0:T(8,128)(2,1)} %copy-done, bf16[512,128]{1,0:T(8,128)(2,1)S(1)} %all_gather.7, bf16[2048,128]{1,0:T(8,128)(2,1)S(1)} %bitcast.185, f32[128]{0:T(128)S(1)} %copy-done.6), kind=kOutput, calls=%fused_computation.62 | convolution fusion | flops 269484032 | bytes 3277312 | tf_op jit(solution)/shard_map/dot_general | solution.py:97
  75.5 62.1 %all-reduce = (f32[512]{0:T(512)S(1)}, f32[7,7,128]{2,1,0:T(8,128)S(1)}, f32[128]{0:T(128)S(1)}) all-reduce(f32[512]{0:T(512)S(1)} %get-tuple-element.132, f32[7,7,128]{2,1,0:T(8,128)S(1)} %reshape.62, f32[128]{0:T(128)S(1)} %get-tuple-element.56), channel_id=1, replica_groups=mesh['fsdp'=2,'rows'=8,'cols'=2] {'rows','cols'}, use_global_device_ids=true, to_apply=%region_9.0 | all-reduce | flops 6912 | bytes 55296 | tf_op jit(solution)/shard_map/psum | solution.py:142
  137.6 9.0 %all-reduce.2 = (f32[512]{0:T(512)}, f32[7,7,128]{2,1,0:T(8,128)}, f32[128]{0:T(128)}) all-reduce(f32[512]{0:T(512)S(1)} %get-tuple-element.58, f32[7,7,128]{2,1,0:T(8,128)S(1)} %get-tuple-element.59, f32[128]{0:T(128)S(1)} %get-tuple-element.60), channel_id=1, replica_groups=mesh['fsdp'=2,'rows'=8,'cols'=2] {'fsdp'}, use_global_device_ids=true, to_apply=%region_10.0 | all-reduce | flops 6912 | bytes 55296 | tf_op jit(solution)/shard_map/psum | solution.py:143
  146.8 13.4 %all-reduce.7.cloned.1.call-done = (f32[128,512]{1,0:T(8,128)}, f32[512,128]{1,0:T(8,128)}) async-done(((f32[128,512]{1,0:T(8,128)}, f32[512,128]{1,0:T(8,128)}), (f32[128,512]{1,0:T(8,128)}, f32[512,128]{1,0:T(8,128)})) %all-reduce.7.cloned.1.call-update) | async-done | bytes 524304 | tf_op jit(solution)/shard_map/psum | solution.py:142
  160.3 8.1 %fusion.108 = bf16[1,16,128,128]{3,2,1,0:T(8,128)(2,1)} fusion(f32[128]{0:T(128)S(1)} %get-tuple-element.126, f32[22,134,128]{2,1,0:T(8,128)S(1)} %maximum_convert_fusion.1, f32[128]{0:T(128)S(1)} %get-tuple-element.127, f32[128]{0:T(128)S(1)} %get-tuple-element.80, f32[128]{0:T(128)S(1)} %get-tuple-element.81, f32[128]{0:T(128)S(1)} %get-tuple-element.82, ...), kind=kLoop, calls=%fused_computation.221 | loop fusion | flops 26214400 | bytes 52453888 | tf_op jit(solution)/shard_map/broadcast_in_dim | solution.py:151
  168.4 23.4 %all-reduce.9.cloned.1.call-done = (f32[128,512]{1,0:T(8,128)}, f32[512,128]{1,0:T(8,128)}) async-done(((f32[128,512]{1,0:T(8,128)}, f32[512,128]{1,0:T(8,128)}), (f32[128,512]{1,0:T(8,128)}, f32[512,128]{1,0:T(8,128)})) %all-reduce.9.cloned.1.call-update) | async-done | bytes 524304 | tf_op jit(solution)/shard_map/psum | solution.py:143
  191.8 1.6 constant_dynamic-slice_fusion
  193.4 1.6 constant_dynamic-slice_fusion.1
  (49 shorter events, 13.3 us)
Async XLA Ops:
  7.2 153.1 %all-reduce.7.cloned.1.call-start = ((), (), s32[]{:S(2)}) async-start(), calls=%async_computation | async-start | bytes 1048576 | tf_op jit(solution)/shard_map/psum | solution.py:142
  8.2 12.1 %collective-permute-start = (bf16[3,128,128]{2,1,0:T(8,128)(2,1)S(1)}, bf16[3,128,128]{2,1,0:T(8,128)(2,1)S(1)}, u32[]{:S(2)}, u32[]{:S(2)}) collective-permute-start(bf16[3,128,128]{2,1,0:T(8,128)(2,1)S(1)} %get-tuple-element.77), channel_id=1, source_target_pairs={{0,2},{2,4},{4,6},{6,8},{8,10},{10,12},{12,14},{1,3},{3,5},{5,7},{... | collective-permute-start | bytes 294920 | tf_op jit(solution)/shard_map/ppermute | solution.py:19
  10.6 9.7 %collective-permute-start.1 = (bf16[3,128,128]{2,1,0:T(8,128)(2,1)S(1)}, bf16[3,128,128]{2,1,0:T(8,128)(2,1)S(1)}, u32[]{:S(2)}, u32[]{:S(2)}) collective-permute-start(bf16[3,128,128]{2,1,0:T(8,128)(2,1)S(1)} %get-tuple-element.78), channel_id=1, source_target_pairs={{2,0},{4,2},{6,4},{8,6},{10,8},{12,10},{14,12},{3,1},{5,3},{7,5},{... | collective-permute-start | bytes 294920 | tf_op jit(solution)/shard_map/ppermute | solution.py:20
  21.1 10.9 %collective-permute-start.2 = (bf16[22,3,128]{2,1,0:T(4,128)(2,1)S(1)}, bf16[22,3,128]{2,1,0:T(4,128)(2,1)S(1)}, u32[]{:S(2)}, u32[]{:S(2)}) collective-permute-start(bf16[22,3,128]{2,1,0:T(4,128)(2,1)S(1)} %get-tuple-element.73), channel_id=1, source_target_pairs={{0,1},{2,3},{4,5},{6,7},{8,9},{10,11},{12,13},{14,15},{16,17},{18,... | collective-permute-start | bytes 50696 | tf_op jit(solution)/shard_map/ppermute | solution.py:19
  25.0 7.1 %collective-permute-start.3 = (bf16[22,3,128]{2,1,0:T(4,128)(2,1)S(1)}, bf16[22,3,128]{2,1,0:T(4,128)(2,1)S(1)}, u32[]{:S(2)}, u32[]{:S(2)}) collective-permute-start(bf16[22,3,128]{2,1,0:T(4,128)(2,1)S(1)} %get-tuple-element.74), channel_id=1, source_target_pairs={{1,0},{3,2},{5,4},{7,6},{9,8},{11,10},{13,12},{15,14},{17,16},{19,... | collective-permute-start | bytes 50696 | tf_op jit(solution)/shard_map/ppermute | solution.py:20
  33.3 8.9 %copy-start.4 = (f32[128]{0:T(128)S(1)}, f32[128]{0:T(128)}, u32[]{:S(2)}) copy-start(f32[128]{0:T(128)} %param.13) | copy-start | bytes 1540
  33.3 8.9 %copy-start.5 = (f32[128]{0:T(128)S(1)}, f32[128]{0:T(128)}, u32[]{:S(2)}) copy-start(f32[128]{0:T(128)} %param.14) | copy-start | bytes 1540
  33.3 9.5 %copy-start.7 = (f32[512]{0:T(512)S(1)}, f32[512]{0:T(512)}, u32[]{:S(2)}) copy-start(f32[512]{0:T(512)} %param.16) | copy-start | bytes 6148
  42.9 1.8 copy-start.2
  44.7 16.7 %copy-start = (bf16[2048,512]{1,0:T(8,128)(2,1)}, bf16[2048,512]{1,0:T(8,128)(2,1)S(1)}, u32[]{:S(2)}) copy-start(bf16[2048,512]{1,0:T(8,128)(2,1)S(1)} %get-tuple-element.128) | copy-start | bytes 6291460
  56.8 15.5 %copy-start.1 = (bf16[1,16,128,128]{3,2,1,0:T(8,128)(2,1)S(1)}, bf16[1,16,128,128]{3,2,1,0:T(8,128)(2,1)}, u32[]{:S(2)}) copy-start(bf16[1,16,128,128]{3,2,1,0:T(8,128)(2,1)} %param.10) | copy-start | bytes 1572868
  56.8 15.5 %copy-start.6 = (f32[128]{0:T(128)S(1)}, f32[128]{0:T(128)}, u32[]{:S(2)}) copy-start(f32[128]{0:T(128)} %param.18) | copy-start | bytes 1540
  58.0 4.9 %collective-permute-start.4 = (bf16[3,128,128]{2,1,0:T(8,128)(2,1)S(1)}, bf16[3,128,128]{2,1,0:T(8,128)(2,1)S(1)}, u32[]{:S(2)}, u32[]{:S(2)}) collective-permute-start(bf16[3,128,128]{2,1,0:T(8,128)(2,1)S(1)} %get-tuple-element.75), channel_id=1, source_target_pairs={{0,2},{2,4},{4,6},{6,8},{8,10},{10,12},{12,14},{1,3},{3,5},{5,7},{... | collective-permute-start | bytes 294920 | tf_op jit(solution)/shard_map/ppermute | solution.py:19
  60.1 6.2 %collective-permute-start.5 = (bf16[3,128,128]{2,1,0:T(8,128)(2,1)S(1)}, bf16[3,128,128]{2,1,0:T(8,128)(2,1)S(1)}, u32[]{:S(2)}, u32[]{:S(2)}) collective-permute-start(bf16[3,128,128]{2,1,0:T(8,128)(2,1)S(1)} %get-tuple-element.76), channel_id=1, source_target_pairs={{2,0},{4,2},{6,4},{8,6},{10,8},{12,10},{14,12},{3,1},{5,3},{7,5},{... | collective-permute-start | bytes 294920 | tf_op jit(solution)/shard_map/ppermute | solution.py:20
  62.8 97.5 %copy-start.3 = (bf16[1,16,128,128]{3,2,1,0:T(8,128)(2,1)S(1)}, bf16[1,16,128,128]{3,2,1,0:T(8,128)(2,1)}, u32[]{:S(2)}) copy-start(bf16[1,16,128,128]{3,2,1,0:T(8,128)(2,1)} %param.19) | copy-start | bytes 1572868
  62.9 129.0 %all-reduce.9.cloned.1.call-start = ((), (), s32[]{:S(2)}) async-start(), calls=%async_computation.1 | async-start | bytes 1048576 | tf_op jit(solution)/shard_map/psum | solution.py:143
  66.3 80.3 %collective-permute-start.6 = (bf16[22,3,128]{2,1,0:T(4,128)(2,1)S(1)}, bf16[22,3,128]{2,1,0:T(4,128)(2,1)S(1)}, u32[]{:S(2)}, u32[]{:S(2)}) collective-permute-start(bf16[22,3,128]{2,1,0:T(4,128)(2,1)S(1)} %get-tuple-element.71), channel_id=1, source_target_pairs={{0,1},{2,3},{4,5},{6,7},{8,9},{10,11},{12,13},{14,15},{16,17},{18,... | collective-permute-start | bytes 50696 | tf_op jit(solution)/shard_map/ppermute | solution.py:19
  71.0 75.6 %collective-permute-start.7 = (bf16[22,3,128]{2,1,0:T(4,128)(2,1)S(1)}, bf16[22,3,128]{2,1,0:T(4,128)(2,1)S(1)}, u32[]{:S(2)}, u32[]{:S(2)}) collective-permute-start(bf16[22,3,128]{2,1,0:T(4,128)(2,1)S(1)} %get-tuple-element.72), channel_id=1, source_target_pairs={{1,0},{3,2},{5,4},{7,6},{9,8},{11,10},{13,12},{15,14},{17,16},{19,... | collective-permute-start | bytes 50696 | tf_op jit(solution)/shard_map/ppermute | solution.py:20
Sparse Core Ops, SparseCore 0:
  63.0 97.2 all-reduce.6
  162.6 29.1 all-reduce.8
